TPU v7x, 32 devices: a whole 2x2x4 slice. The times are simulated.
32 devices in a mesh: groups: 2 (over y), wide: 8 (over z, x), narrow: 2 (over core).
Axes of the slice: x: 2, y: 2, z: 4, core: 2. Of those that a mesh axis runs over, the one named last changes fastest.
Arguments:
- goals: float32 [8192, 1024], P(('groups', 'wide', 'narrow')), parts along dimension 0, may hold values from -32 to 32
- premises: float32 [1024, 1024], P(('groups', 'wide', 'narrow')), parts along dimension 0, may hold values from -24 to 24
- counts: int32 [8192], P(('groups', 'wide')), parts along dimension 0, may hold values from 1 to 16
- positives: int32 [8192, 16], P(('groups', 'wide')), parts along dimension 0, may hold values from -1 to 511, as said below
- cotangent: float32 [8192], P(('groups', 'wide')), parts along dimension 0, may hold values from -6 to 6
Outputs:
- goal_loss: float32 [8192], P(('groups', 'wide')), parts along dimension 0
- grad_goals: float32 [8192, 1024], P(('groups', 'wide', 'narrow')), parts along dimension 0
- grad_premises: float32 [1024, 1024], P(('groups', 'wide', 'narrow')), parts along dimension 0
There are 2 independent parts, one for each index of `groups`. A program takes and returns all parts, laid end to end along the dimension named above; each array names one. Nothing has to cross between parts.
Inputs may be any that keep to these rules, and one draw needn't show every extreme that they name: positives[i, k] is a premise index for k < counts[i] and -1 from there on.
All inputs are finite; a program needn't handle non-finite values.
Results may differ from a plain program's by a relative error of at most 0.012.
The roundings to bfloat16 on the way count: a program that leaves them out, or rounds other values in their place, can miss the bound.
Values may be sent and summed in bfloat16 or wider, within the bound.
A program may use at most 64 MiB of HBM per device.

v0:
```python
import jax
import jax.numpy as jnp
from jax import lax
from jax.sharding import PartitionSpec as P


def hit_counts(row_lists, column_ids):
    total = jnp.zeros((row_lists.shape[0], column_ids.shape[0]), jnp.float32)
    for which_slot in range(row_lists.shape[1]):
        total = total + (row_lists[:, which_slot][:, None] == column_ids[None, :]).astype(
            jnp.float32
        )
    return total


def per_device(goals, premises, counts, positives, cotangent):
    goal_part = goals.astype(jnp.bfloat16)
    prem_part = premises.astype(jnp.bfloat16)
    prem_rows = prem_part.shape[0]
    width = goal_part.shape[1]
    scale = width ** (-0.5)
    n_wide = lax.axis_size("wide")
    n_narrow = lax.axis_size("narrow")
    narrow_index = lax.axis_index("narrow")
    rows_block = lax.all_gather(goal_part, "narrow", axis=0, tiled=True)
    prem_block = lax.all_gather(prem_part, "wide", axis=0, tiled=True)
    goal_counts = counts.astype(jnp.float32)
    local_ids = jnp.arange(prem_rows * n_wide, dtype=jnp.int32)
    column_ids = (
        local_ids // prem_rows * n_narrow + narrow_index
    ) * prem_rows + local_ids % prem_rows
    col_total = prem_block.shape[0]
    row_total = rows_block.shape[0]
    step_cols = 512 if col_total % 512 == 0 else col_total
    starts = list(range(0, col_total, step_cols))

    def tile_scores(begin):
        piece = prem_block[begin : begin + step_cols]
        return (
            lax.dot_general(
                rows_block, piece, (((1,), (1,)), ((), ())), preferred_element_type=jnp.float32
            )
            * scale
        )

    top = jnp.full((row_total,), -jnp.inf, jnp.float32)
    total = jnp.zeros((row_total,), jnp.float32)
    positive_sum = jnp.zeros((row_total,), jnp.float32)
    for begin in starts:
        scores = tile_scores(begin)
        hits = hit_counts(positives, column_ids[begin : begin + step_cols])
        new_top = jnp.maximum(top, jnp.max(scores, axis=1))
        total = total * jnp.exp(top - new_top) + jnp.sum(jnp.exp(scores - new_top[:, None]), axis=1)
        positive_sum = positive_sum + jnp.sum(hits * scores, axis=1)
        top = new_top
    best = lax.pmax(top, "narrow")
    total_all, positive_all = lax.psum((total * jnp.exp(top - best), positive_sum), "narrow")
    log_total = best + jnp.log(total_all)
    row_loss = log_total - positive_all / goal_counts
    grad_rows = jnp.zeros((row_total, width), jnp.float32)
    pieces = []
    for number, begin in enumerate(starts):
        scores = tile_scores(begin)
        hits = hit_counts(positives, column_ids[begin : begin + step_cols])
        dscores = (
            cotangent[:, None]
            * (jnp.exp(scores - log_total[:, None]) - hits / goal_counts[:, None])
            * scale
        ).astype(jnp.bfloat16)
        grad_rows = grad_rows + jnp.dot(
            dscores, prem_block[begin : begin + step_cols], preferred_element_type=jnp.float32
        )
        pieces.append(dscores)
    stored = jnp.concatenate(pieces, axis=1)
    grad_goals = lax.psum_scatter(grad_rows, "narrow", scatter_dimension=0, tiled=True)
    grad_premises = lax.psum_scatter(
        lax.dot_general(
            stored, rows_block, (((0,), (0,)), ((), ())), preferred_element_type=jnp.float32
        ),
        "wide",
        scatter_dimension=0,
        tiled=True,
    )
    return (row_loss, grad_goals, grad_premises)


def solution(mesh):
    return jax.shard_map(
        per_device,
        mesh=mesh,
        in_specs=(
            P(("groups", "wide", "narrow"), None),
            P(("groups", "wide", "narrow"), None),
            P(("groups", "wide")),
            P(("groups", "wide"), None),
            P(("groups", "wide")),
        ),
        out_specs=(
            P(("groups", "wide")),
            P(("groups", "wide", "narrow"), None),
            P(("groups", "wide", "narrow"), None),
        ),
        check_vma=False,
    )
```

profile of v0, /device:TPU:0, one launch (start us, length us, event | category | flops | bytes accessed | tf_op | source)
XLA Modules:
  0.0 136.1 jit_solution(13301415830657365863)
XLA Ops:
  7.2 0.0 copy-start.2
  7.2 0.0 copy-start
  7.2 0.0 copy-start.1
  7.2 0.0 all-gather.2.cloned.1.call-start
  7.2 2.1 %convert_element_type.76 = bf16[256,1024]{1,0:T(8,128)(2,1)} convert(f32[256,1024]{1,0:T(8,128)} %param.5) | non-fusion elementwise | flops 262144 | bytes 1572864 | tf_op jit(solution)/shard_map/convert_element_type | solution.py:17
  9.4 0.0 copy-start.4
  9.4 0.0 all-gather.2.cloned.1.call-update
  9.4 0.0 reduce-scatter.5.cloned.1.call-start
  9.4 0.0 copy-done.2
  9.5 0.0 copy-done
  9.5 0.0 copy-done.1
  9.6 33.0 %all_gather.7 = bf16[256,1024]{1,0:T(8,128)(2,1)S(1)} all-gather(bf16[32,1024]{1,0:T(8,128)(2,1)S(1)} %convert_element_type.77), channel_id=1, replica_groups=mesh['groups'=2,'wide'=8,'narrow'=2] {'wide'}, dimensions={0}, use_global_device_ids=true | all-gather | bytes 589824 | tf_op jit(solution)/shard_map/all_gather | solution.py:26
  42.6 0.0 all-gather.2.cloned.1.call-done
  42.6 0.0 copy-start.3
  42.6 1.8 %fusion.9 = (f32[512]{0:T(512)S(1)}, f32[512,256]{0,1:T(8,128)S(1)}) fusion(bf16[512,1024]{1,0:T(8,128)(2,1)} %all-gather.2.cloned.1.call-done, bf16[256,1024]{1,0:T(8,128)(2,1)S(1)} %all_gather.7), kind=kOutput, calls=%fused_computation.22 | convolution fusion | flops 268697088 | bytes 2099200 | tf_op jit(solution)/shard_map/dot_general | solution.py:40
  44.4 2.5 %pmax.7 = f32[512]{0:T(512)S(1)} all-reduce(f32[512]{0:T(512)S(1)} %get-tuple-element.25), channel_id=1, replica_groups=mesh['groups'=2,'wide'=8,'narrow'=2] {'narrow'}, use_global_device_ids=true, to_apply=%region_1.2 | all-reduce | flops 512 | bytes 4096 | tf_op jit(solution)/shard_map/pmax | solution.py:56
  46.9 1.1 multiply_reduce_fusion
  47.9 2.5 %all-reduce = (f32[512]{0:T(512)S(1)}, f32[512]{0:T(512)S(1)}) all-reduce(f32[512]{0:T(512)S(1)} %exponential_multiply_fusion, f32[512]{0:T(512)S(1)} %get-tuple-element.3), channel_id=1, replica_groups=mesh['groups'=2,'wide'=8,'narrow'=2] {'narrow'}, use_global_device_ids=true, to_apply=%region_3.4 | all-reduce | flops 1024 | bytes 8192 | tf_op jit(solution)/shard_map/psum | solution.py:57
  50.4 0.6 divide_subtract_fusion
  51.0 0.0 copy-done.4
  51.0 0.0 copy-done.3
  51.0 2.3 %fusion.6 = f32[256,1024]{1,0:T(8,128)} fusion(bf16[512,1024]{1,0:T(8,128)(2,1)S(1)} %copy-done.3, f32[512,256]{0,1:T(8,128)S(1)} %get-tuple-element.26, f32[512]{0:T(512)S(1)} %convert_element_type.94, f32[512]{0:T(512)S(1)} %get-tuple-element.8, f32[512]{0:T(512)S(1)} %copy-done.4, s32[512]{0:T(512)S(1)} %bitcast.63, s32[512]{0:T(512)S(1)} %bitcast.66, ...), kind=kOutput, calls=%fused_computation.19 | convolution fusion | flops 275382272 | bytes 2661376 | tf_op jit(solution)/shard_map/dot_general | solution.py:77
  53.3 0.0 reduce-scatter.5.cloned.1.call-update
  53.3 0.0 reduce-scatter.3.cloned.1.call-start
  53.4 2.7 %fusion.7 = f32[512,1024]{1,0:T(8,128)} fusion(bf16[256,1024]{1,0:T(8,128)(2,1)S(1)} %all_gather.7, f32[512,256]{0,1:T(8,128)S(1)} %get-tuple-element.26, f32[512]{0:T(512)S(1)} %convert_element_type.94, f32[512]{0:T(512)S(1)} %get-tuple-element.8, f32[512]{0:T(512)S(1)} %copy-done.4, s32[512]{0:T(512)S(1)} %bitcast.64, s32[512]{0:T(512)S(1)} %bitcast.67, ...), kind=kOutput, calls=%fused_computation.20 | convolution fusion | flops 275382272 | bytes 3185664 | tf_op jit(solution)/shard_map/dot_general | solution.py:70
  56.1 0.0 reduce-scatter.3.cloned.1.call-update
  56.1 61.9 %reduce-scatter.5.cloned.1.call-done = f32[32,1024]{1,0:T(8,128)} async-done(((f32[256,1024]{1,0:T(8,128)}), f32[32,1024]{1,0:T(8,128)}) %reduce-scatter.5.cloned.1.call-update) | async-done | bytes 131088 | tf_op jit(solution)/shard_map/reduce_scatter | solution.py:76
  118.0 11.6 %reduce-scatter.3.cloned.1.call-done = f32[256,1024]{1,0:T(8,128)} async-done(((f32[512,1024]{1,0:T(8,128)}), f32[256,1024]{1,0:T(8,128)}) %reduce-scatter.3.cloned.1.call-update) | async-done | bytes 1048592 | tf_op jit(solution)/shard_map/reduce_scatter | solution.py:75
  (5 shorter events, 0.1 us)
Async XLA Ops:
  7.2 2.3 %copy-start.2 = (s32[512]{0:T(512)S(1)}, s32[512]{0:T(512)}, u32[]{:S(2)}) copy-start(s32[512]{0:T(512)} %param.7) | copy-start | bytes 6148
  7.2 2.3 %copy-start = (f32[32,1024]{1,0:T(8,128)S(1)}, f32[32,1024]{1,0:T(8,128)}, u32[]{:S(2)}) copy-start(f32[32,1024]{1,0:T(8,128)} %param.6) | copy-start | bytes 393220
  7.2 2.3 %copy-start.1 = (s32[512,16]{0,1:T(8,128)S(1)}, s32[512,16]{0,1:T(8,128)}, u32[]{:S(2)}) copy-start(s32[512,16]{0,1:T(8,128)} %param.8) | copy-start | bytes 98308
  7.2 35.4 %all-gather.2.cloned.1.call-start = ((), (), s32[]{:S(2)}) async-start(), calls=%async_computation.2 | async-start | bytes 1572864 | tf_op jit(solution)/shard_map/all_gather | solution.py:25
  9.4 41.6 %copy-start.4 = (f32[512]{0:T(512)S(1)}, f32[512]{0:T(512)}, u32[]{:S(2)}) copy-start(f32[512]{0:T(512)} %param.9) | copy-start | bytes 6148
  9.4 108.6 %reduce-scatter.5.cloned.1.call-start = ((), (), s32[]{:S(2)}) async-start(), calls=%async_computation.4 | async-start | bytes 1179648 | tf_op jit(solution)/shard_map/reduce_scatter | solution.py:76
  42.6 8.4 %copy-start.3 = (bf16[512,1024]{1,0:T(8,128)(2,1)S(1)}, bf16[512,1024]{1,0:T(8,128)(2,1)}, u32[]{:S(2)}) copy-start(bf16[512,1024]{1,0:T(8,128)(2,1)} %all-gather.2.cloned.1.call-done) | copy-start | bytes 3145732
  53.3 76.3 %reduce-scatter.3.cloned.1.call-start = ((), (), s32[]{:S(2)}) async-start(), calls=%async_computation.3 | async-start | bytes 3145728 | tf_op jit(solution)/shard_map/reduce_scatter | solution.py:75
Sparse Core Ops, SparseCore 0:
  10.1 11.7 all-gather.1
  53.4 64.5 reduce-scatter.4
  120.9 8.6 reduce-scatter.2
where the time goes:
time: 136 us
  waiting for transfers between devices  73.5 us (54%)
  blocking collectives  38 us (28%)
  between operations  13.8 us (10%)
  matrix products  6.82 us (5%)
  other arithmetic  3.82 us (3%)
    reduce_scatter x1, waiting for transfers between devices, per_device(): lax.psum_scatter(lax.dot_general(stored, rows_block, (((0,), (0,)), ((),...  61.9 us
    all_gather x1, blocking collectives, per_device(): prem_block = lax.all_gather(prem_part, 'wide', axis=0, tiled=True)  33 us
    reduce_scatter x1, waiting for transfers between devices, per_device(): lax.psum_scatter(grad_rows, 'narrow', scatter_dimension=0, tiled=True)  11.6 us
    dot_general x1, matrix products, per_device(): jnp.dot(dscores, prem_block[begin:begin + step_cols], preferred_element_t...  2.73 us
  transfers between devices with their start and end apart: 3, of which 2 were waited for; matrix products, arithmetic and copies ran while one was open for 2% of the time, Pallas kernels for 0%

commit v1 on v0

v1 whole, which is shorter than its diff:
```python
import functools

import jax
import jax.numpy as jnp
from jax import lax
from jax.experimental import pallas as pl
from jax.experimental.pallas import tpu as pltpu
from jax.sharding import PartitionSpec as P

MESH = pl.DeviceIdType.MESH


def kernel(
    n_hi,
    n_lo,
    goals_hbm,
    prem_hbm,
    counts_ref,
    positives_ref,
    cot_ref,
    loss_ref,
    dgoal_hbm,
    dprem_ref,
    goals_in,
    prem_in,
    goals_all,
    prem_all,
    weights,
    scores,
    dscores,
    dgoal,
    dprem,
    lo_out,
    lo_in,
    hi_out,
    hi_in,
    local_sems,
    goal_sems,
    ag_send,
    ag_recv,
    fwd_send,
    fwd_recv,
    lo_send,
    lo_recv,
    hi_send,
    hi_recv,
):
    group = lax.axis_index("groups")
    wide = lax.axis_index("wide")
    narrow = lax.axis_index("narrow")
    n_wide = n_hi * n_lo
    hi = wide // n_lo
    lo = wide % n_lo
    rows, width = prem_in.shape
    own_goals = goals_in.shape[0]
    half = n_wide * rows
    scale = width ** (-0.5)

    def hi_peer(a):
        return ((hi + a) % n_hi) * n_lo + lo

    def lo_peer(b):
        return hi * n_lo + (lo + b) % n_lo

    def at(w, n):
        return (group, w, n)

    barrier = pltpu.get_barrier_semaphore()
    for a in range(1, n_hi):
        pl.semaphore_signal(barrier, inc=1, device_id=at(hi_peer(a), narrow), device_id_type=MESH)
    for b in range(1, n_lo):
        pl.semaphore_signal(barrier, inc=1, device_id=at(lo_peer(b), narrow), device_id_type=MESH)
    pl.semaphore_signal(barrier, inc=1, device_id=at(wide, 1 - narrow), device_id_type=MESH)

    load_prem = pltpu.make_async_copy(prem_hbm, prem_in, local_sems.at[0])
    load_prem.start()
    load_goals = pltpu.make_async_copy(goals_hbm, goals_in, local_sems.at[1])
    load_goals.start()

    def block(owner_wide, part):
        start = pl.multiple_of(part * half + owner_wide * rows, rows)
        return prem_all.at[pl.ds(start, rows), :]

    def source(a, b):
        return ((hi + n_hi - a) % n_hi) * n_lo + (lo + n_lo - b) % n_lo

    def hi_copy(a, owner):
        return pltpu.make_async_remote_copy(
            src_ref=block(owner, 0),
            dst_ref=block(owner, 0),
            send_sem=ag_send.at[a * n_lo],
            recv_sem=ag_recv.at[a * n_lo],
            device_id=at(hi_peer(a), narrow),
            device_id_type=MESH,
        )

    def lo_copy(a, b, owner):
        return pltpu.make_async_remote_copy(
            src_ref=block(owner, 0),
            dst_ref=block(owner, 0),
            send_sem=ag_send.at[a * n_lo + b],
            recv_sem=ag_recv.at[a * n_lo + b],
            device_id=at(lo_peer(b), narrow),
            device_id_type=MESH,
        )

    def forward(a, b, owner):
        return pltpu.make_async_remote_copy(
            src_ref=block(owner, 0),
            dst_ref=block(owner, 1),
            send_sem=fwd_send.at[a * n_lo + b],
            recv_sem=fwd_recv.at[a * n_lo + b],
            device_id=at(wide, 1 - narrow),
            device_id_type=MESH,
        )

    load_prem.wait()
    prem_all[pl.ds(pl.multiple_of(wide * rows, rows), rows), :] = prem_in[...].astype(jnp.bfloat16)
    pl.semaphore_wait(barrier, n_hi - 1 + n_lo - 1 + 1)
    for a in range(n_hi - 1, 0, -1):
        hi_copy(a, wide).start()
    for b in range(1, n_lo):
        lo_copy(0, b, wide).start()
    forward(0, 0, wide).start()

    load_goals.wait()
    own_rows = pl.ds(pl.multiple_of(narrow * own_goals, own_goals), own_goals)
    goals_all[own_rows, :] = goals_in[...].astype(jnp.bfloat16)
    goal_copy = pltpu.make_async_remote_copy(
        src_ref=goals_all.at[own_rows, :],
        dst_ref=goals_all.at[own_rows, :],
        send_sem=goal_sems.at[0],
        recv_sem=goal_sems.at[1],
        device_id=at(wide, 1 - narrow),
        device_id_type=MESH,
    )
    goal_copy.start()

    all_goals = goals_all.shape[0]
    lists = positives_ref[...]
    inverse = 1.0 / counts_ref[...].astype(jnp.float32)
    step = 64

    def weigh(number, carry):
        begin = pl.multiple_of(number * step, step)
        local = begin + lax.broadcasted_iota(jnp.int32, (step, all_goals), 0)
        part = local // half
        inner = local - part * half
        owner = inner // rows
        side = narrow + part * (1 - 2 * narrow)
        ids = (owner * 2 + side) * rows + inner % rows
        total = jnp.zeros((step, all_goals), jnp.float32)
        for slot in range(lists.shape[0]):
            total = total + jnp.where(lists[slot : slot + 1, :] == ids, 1.0, 0.0)
        weights[pl.ds(begin, step), :] = total * inverse
        return carry

    lax.fori_loop(0, 2 * half // step, weigh, 0)

    for a in range(1, n_hi):
        owner = source(a, 0)
        hi_copy(a, owner).wait_recv()
        for b in range(1, n_lo):
            lo_copy(a, b, owner).start()
        forward(a, 0, owner).start()
    for a in range(n_hi):
        for b in range(1, n_lo):
            owner = source(a, b)
            lo_copy(a, b, owner).wait_recv()
            forward(a, b, owner).start()
    goal_copy.wait()

    tall = min(256, half)

    def score(begin):
        span = pl.ds(pl.multiple_of(begin, tall), tall)
        scores[span, :] = (
            lax.dot_general(
                prem_all[span, :],
                goals_all[...],
                (((1,), (1,)), ((), ())),
                preferred_element_type=jnp.float32,
            )
            * scale
        )

    pl.loop(0, half // tall)(lambda number: score(number * tall))
    for a in range(n_hi):
        for b in range(n_lo):
            forward(a, b, source(a, b)).wait_recv()
    pl.loop(0, half // tall)(lambda number: score(half + number * tall))

    lanes = 128

    def soften(number, carry):
        cols = pl.ds(pl.multiple_of(number * lanes, lanes), lanes)
        tile = scores[:, cols]
        weight = weights[:, cols]
        top = jnp.max(tile, axis=0, keepdims=True)
        powers = jnp.exp(tile - top)
        total = jnp.sum(powers, axis=0, keepdims=True)
        positive = jnp.sum(weight * tile, axis=0, keepdims=True)
        loss_ref[:, cols] = top + jnp.log(total) - positive
        factor = cot_ref[:, cols] * scale
        dscores[:, cols] = (factor * (powers * (1.0 / total) - weight)).astype(jnp.bfloat16)
        return carry

    lax.fori_loop(0, all_goals // lanes, soften, 0)

    def premise_gradient(number):
        span = pl.ds(pl.multiple_of(number * tall, tall), tall)
        piece = jnp.dot(dscores[span, :], goals_all[...], preferred_element_type=jnp.float32)
        dprem[span, :] = piece
        lo_out[span, :] = piece.astype(jnp.bfloat16)

    pl.loop(0, half // tall)(premise_gradient)

    def lo_reduce(a, b):
        target_hi = (hi + a) % n_hi
        target = target_hi * n_lo + (lo + b) % n_lo
        return pltpu.make_async_remote_copy(
            src_ref=lo_out.at[pl.ds(pl.multiple_of(target * rows, rows), rows), :],
            dst_ref=lo_in.at[a * n_lo + b],
            send_sem=lo_send.at[a * n_lo + b],
            recv_sem=lo_recv.at[a * n_lo + b],
            device_id=at(lo_peer(b), narrow),
            device_id_type=MESH,
        )

    def hi_reduce(a):
        return pltpu.make_async_remote_copy(
            src_ref=hi_out.at[a],
            dst_ref=hi_in.at[a],
            send_sem=hi_send.at[a],
            recv_sem=hi_recv.at[a],
            device_id=at(hi_peer(a), narrow),
            device_id_type=MESH,
        )

    order = list(range(1, n_hi)) + [0]
    for a in order:
        for b in range(1, n_lo):
            lo_reduce(a, b).start()

    def pair_sum(a):
        target = hi_peer(a)
        total = dprem[pl.ds(pl.multiple_of(target * rows, rows), rows), :]
        for b in range(1, n_lo):
            lo_reduce(a, b).wait_recv()
            total = total + lo_in[a * n_lo + b].astype(jnp.float32)
        return total

    if n_lo == 1:
        for a in range(1, n_hi):
            hi_out[a] = pair_sum(a).astype(jnp.bfloat16)
            hi_reduce(a).start()

    dgoal[...] = lax.dot_general(
        dscores[:, pl.ds(pl.multiple_of(narrow * own_goals, own_goals), own_goals)],
        prem_all[...],
        (((0,), (0,)), ((), ())),
        preferred_element_type=jnp.float32,
    )
    store_goals = pltpu.make_async_copy(dgoal, dgoal_hbm, local_sems.at[2])
    store_goals.start()

    if n_lo > 1:
        for a in range(1, n_hi):
            hi_out[a] = pair_sum(a).astype(jnp.bfloat16)
            hi_reduce(a).start()
    mine = pair_sum(0)
    for a in range(1, n_hi):
        hi_reduce(a).wait_recv()
        mine = mine + hi_in[a].astype(jnp.float32)
    dprem_ref[...] = mine

    for a in range(1, n_hi):
        hi_copy(a, wide).wait_send()
        hi_reduce(a).wait_send()
    for a in range(n_hi):
        for b in range(1, n_lo):
            lo_copy(a, b, source(a, 0)).wait_send()
            lo_reduce(a, b).wait_send()
        for b in range(n_lo):
            forward(a, b, source(a, b)).wait_send()
    store_goals.wait()


def per_device(n_wide, goals, premises, counts, positives, cotangent):
    n_lo = 2 if n_wide % 2 == 0 else 1
    n_hi = n_wide // n_lo
    own_goals, width = goals.shape
    rows = premises.shape[0]
    all_goals = counts.shape[0]
    half = n_wide * rows
    bf16, f32 = jnp.bfloat16, jnp.float32
    vmem = pl.BlockSpec(memory_space=pltpu.VMEM)
    anywhere = pl.BlockSpec(memory_space=pl.ANY)
    dma = pltpu.SemaphoreType.DMA
    scratch = [
        pltpu.VMEM((own_goals, width), f32),
        pltpu.VMEM((rows, width), f32),
        pltpu.VMEM((all_goals, width), bf16),
        pltpu.VMEM((2 * half, width), bf16),
        pltpu.VMEM((2 * half, all_goals), f32),
        pltpu.VMEM((2 * half, all_goals), f32),
        pltpu.VMEM((2 * half, all_goals), bf16),
        pltpu.VMEM((own_goals, width), f32),
        pltpu.VMEM((half, width), f32),
        pltpu.VMEM((half, width), bf16),
        pltpu.VMEM((n_wide, rows, width), bf16),
        pltpu.VMEM((n_hi, rows, width), bf16),
        pltpu.VMEM((n_hi, rows, width), bf16),
        dma((3,)),
        dma((2,)),
        dma((n_wide,)),
        dma((n_wide,)),
        dma((n_wide,)),
        dma((n_wide,)),
        dma((n_wide,)),
        dma((n_wide,)),
        dma((n_hi,)),
        dma((n_hi,)),
    ]
    loss, dgoal, dprem = pl.pallas_call(
        functools.partial(kernel, n_hi, n_lo),
        out_shape=(
            jax.ShapeDtypeStruct((1, all_goals), f32),
            jax.ShapeDtypeStruct((own_goals, width), f32),
            jax.ShapeDtypeStruct((rows, width), f32),
        ),
        in_specs=[anywhere, anywhere, vmem, vmem, vmem],
        out_specs=(vmem, anywhere, vmem),
        scratch_shapes=scratch,
        compiler_params=pltpu.CompilerParams(
            collective_id=0, has_side_effects=True, vmem_limit_bytes=58 * 1024 * 1024
        ),
    )(goals, premises, counts.reshape(1, all_goals), positives.T, cotangent.reshape(1, all_goals))
    return (loss.reshape(all_goals), dgoal, dprem)


def solution(mesh):
    return jax.shard_map(
        functools.partial(per_device, mesh.shape["wide"]),
        mesh=mesh,
        in_specs=(
            P(("groups", "wide", "narrow"), None),
            P(("groups", "wide", "narrow"), None),
            P(("groups", "wide")),
            P(("groups", "wide"), None),
            P(("groups", "wide")),
        ),
        out_specs=(
            P(("groups", "wide")),
            P(("groups", "wide", "narrow"), None),
            P(("groups", "wide", "narrow"), None),
        ),
        check_vma=False,
    )
```

time: 136 us -> 36.8 us (0.27)
  waiting for transfers between devices: 73.5 us -> 0 us
  blocking collectives: 38 us -> 0 us
  Pallas kernels: 0 us -> 31.7 us
  between operations: 13.8 us -> 0.65 us
  matrix products: 6.82 us -> 0 us
  local copies, waits for them, and re-layouts: 0.05 us -> 4.25 us
  other arithmetic: 3.82 us -> 0 us
    reduce_scatter x2 -> x0, waiting for transfers between devices: 73.5 us -> none  [the longest x1 61.9 us: per_device(): lax.psum_scatter(lax.dot_general(stored, rows_block, (((0,), (0,)), ((),...]
    all_gather x1 -> x0, blocking collectives: 33 us -> none  [per_device(): prem_block = lax.all_gather(prem_part, 'wide', axis=0, tiled=True)]
    pallas_call x0 -> x1, Pallas kernels: none -> 31.7 us  [per_device(): pl.pallas_call(functools.partial(kernel, n_hi, n_lo), out_shape=(jax.Shap...]
    dot_general x3 -> x0, matrix products: 6.82 us -> none  [the longest x1 2.73 us: per_device(): jnp.dot(dscores, prem_block[begin:begin + step_cols], preferred_element_t...]
    unnamed x10 -> x7, local copies, waits for them, and re-layouts: 0.02 us -> 4.25 us
    pmax x1 -> x0, blocking collectives: 2.47 us -> none  [per_device(): best = lax.pmax(top, 'narrow')]
    psum x1 -> x0, blocking collectives: 2.47 us -> none  [per_device(): lax.psum((total * jnp.exp(top - best), positive_sum), 'narrow')]
    convert_element_type x3 -> x0, other arithmetic: 2.14 us -> none  [the longest x1 2.12 us: per_device(): goal_part = goals.astype(jnp.bfloat16)]
  transfers between devices with their start and end apart: 3 -> 0, of which waited for: 2 -> 0; matrix products, arithmetic and copies ran while one was open for 2% -> 0% of each run, Pallas kernels for 0% -> 0%
where the time goes in v1:
time: 36.8 us; the launch traced here: 36.6 us
  Pallas kernels  31.7 us (86%)
  local copies, waits for them, and re-layouts  4.25 us (12%)
  between operations  0.65 us (2%)
    pallas_call x1, Pallas kernels, per_device(): pl.pallas_call(functools.partial(kernel, n_hi, n_lo), out_shape=(jax.Shap...  31.7 us
    unnamed x7, local copies, waits for them, and re-layouts  4.25 us

profile of v1, /device:TPU:0, one launch (start us, length us, event | category | flops | bytes accessed | tf_op | source)
XLA Modules:
  0.0 36.6 jit_solution(15972506816952145314)
XLA Ops:
  0.6 31.7 %shard_map.76 = (f32[1,512]{1,0:T(1,128)}, f32[256,1024]{1,0:T(8,128)}, f32[32,1024]{1,0:T(8,128)}) custom-call(f32[256,1024]{1,0:T(8,128)} %goals_hbm.1, f32[32,1024]{1,0:T(8,128)} %prem_hbm.1, s32[1,512]{1,0:T(1,128)} %bitcast.5, s32[16,512]{1,0:T(8,128)} %bitcast.4, f32[1,512]{1,0:T(1,128)} %bitcast.6), custom_call_target="tpu_custom_call" | custom-call | tf_op jit(solution)/shard_map/pallas_call | solution.py:325
  32.3 0.0 copy-start.1
  32.3 0.7 %copy-done.1 = f32[1,512]{1,0:T(1,128)S(1)} copy-done((f32[1,512]{1,0:T(1,128)S(1)}, f32[1,512]{1,0:T(1,128)}, u32[]{:S(2)}) %copy-start.1) | copy-done | bytes 2072
  33.0 0.6 %copy.11 = f32[512]{0:T(512)} copy(f32[512]{0:T(512)S(1)} %bitcast.7) | data formatting | bytes 4096
  33.6 0.0 copy-start
  33.6 2.3 %copy.12 = f32[256,1024]{1,0:T(8,128)} copy(f32[256,1024]{1,0:T(8,128)} %get-tuple-element.13) | data formatting | bytes 2097152
  35.9 0.0 copy-done
  35.9 0.7 %copy.13 = f32[32,1024]{1,0:T(8,128)} copy(f32[32,1024]{1,0:T(8,128)S(1)} %copy-done) | data formatting | bytes 262144
Async XLA Ops:
  32.3 0.7 %copy-start.1 = (f32[1,512]{1,0:T(1,128)S(1)}, f32[1,512]{1,0:T(1,128)}, u32[]{:S(2)}) copy-start(f32[1,512]{1,0:T(1,128)} %get-tuple-element.6) | copy-start | bytes 6148
  33.6 2.3 %copy-start = (f32[32,1024]{1,0:T(8,128)S(1)}, f32[32,1024]{1,0:T(8,128)}, u32[]{:S(2)}) copy-start(f32[32,1024]{1,0:T(8,128)} %get-tuple-element.14) | copy-start | bytes 393220

commit v2 on v1

--- a/solution.py
+++ b/solution.py
@@ -15,20 +15,22 @@
     n_lo,
     goals_hbm,
     prem_hbm,
+    counts_hbm,
+    positives_hbm,
+    cot_hbm,
+    loss_ref,
+    dgoal,
+    dprem_ref,
+    goals_in,
+    prem_in,
     counts_ref,
     positives_ref,
     cot_ref,
-    loss_ref,
-    dgoal_hbm,
-    dprem_ref,
-    goals_in,
-    prem_in,
     goals_all,
     prem_all,
     weights,
     scores,
     dscores,
-    dgoal,
     dprem,
     lo_out,
     lo_in,
@@ -62,6 +64,14 @@
     def lo_peer(b):
         return hi * n_lo + (lo + b) % n_lo
 
+    odd = hi % 2
+    if n_hi == 4:
+        near_first = [1 + 2 * odd, 3 - 2 * odd, 2]
+        arrive_first = [3 - 2 * odd, 1 + 2 * odd, 2]
+        far_first = [2, 3 - 2 * odd, 1 + 2 * odd]
+    else:
+        near_first = arrive_first = far_first = list(range(1, n_hi))
+
     def at(w, n):
         return (group, w, n)
 
@@ -76,6 +86,13 @@
     load_prem.start()
     load_goals = pltpu.make_async_copy(goals_hbm, goals_in, local_sems.at[1])
     load_goals.start()
+    small = [(counts_hbm, counts_ref), (positives_hbm, positives_ref), (cot_hbm, cot_ref)]
+    small_loads = [
+        pltpu.make_async_copy(src, dst, local_sems.at[2 + number])
+        for number, (src, dst) in enumerate(small)
+    ]
+    for load in small_loads:
+        load.start()
 
     def block(owner_wide, part):
         start = pl.multiple_of(part * half + owner_wide * rows, rows)
@@ -117,10 +134,10 @@
     load_prem.wait()
     prem_all[pl.ds(pl.multiple_of(wide * rows, rows), rows), :] = prem_in[...].astype(jnp.bfloat16)
     pl.semaphore_wait(barrier, n_hi - 1 + n_lo - 1 + 1)
-    for a in range(n_hi - 1, 0, -1):
-        hi_copy(a, wide).start()
     for b in range(1, n_lo):
         lo_copy(0, b, wide).start()
+    for a in near_first:
+        hi_copy(a, wide).start()
     forward(0, 0, wide).start()
 
     load_goals.wait()
@@ -137,6 +154,8 @@
     goal_copy.start()
 
     all_goals = goals_all.shape[0]
+    for load in small_loads:
+        load.wait()
     lists = positives_ref[...]
     inverse = 1.0 / counts_ref[...].astype(jnp.float32)
     step = 64
@@ -157,13 +176,13 @@
 
     lax.fori_loop(0, 2 * half // step, weigh, 0)
 
-    for a in range(1, n_hi):
+    for a in arrive_first:
         owner = source(a, 0)
         hi_copy(a, owner).wait_recv()
         for b in range(1, n_lo):
             lo_copy(a, b, owner).start()
         forward(a, 0, owner).start()
-    for a in range(n_hi):
+    for a in [0] + arrive_first:
         for b in range(1, n_lo):
             owner = source(a, b)
             lo_copy(a, b, owner).wait_recv()
@@ -237,8 +256,7 @@
             device_id_type=MESH,
         )
 
-    order = list(range(1, n_hi)) + [0]
-    for a in order:
+    for a in far_first + [0]:
         for b in range(1, n_lo):
             lo_reduce(a, b).start()
 
@@ -261,11 +279,9 @@
         (((0,), (0,)), ((), ())),
         preferred_element_type=jnp.float32,
     )
-    store_goals = pltpu.make_async_copy(dgoal, dgoal_hbm, local_sems.at[2])
-    store_goals.start()
 
     if n_lo > 1:
-        for a in range(1, n_hi):
+        for a in far_first:
             hi_out[a] = pair_sum(a).astype(jnp.bfloat16)
             hi_reduce(a).start()
     mine = pair_sum(0)
@@ -283,7 +299,22 @@
             lo_reduce(a, b).wait_send()
         for b in range(n_lo):
             forward(a, b, source(a, b)).wait_send()
-    store_goals.wait()
+
+
+def publish(loss_in, dgoal_in, dprem_in, loss_out, dgoal_out, dprem_out, sems):
+    pairs = [(loss_in, loss_out), (dprem_in, dprem_out)]
+    pieces = 4
+    tall = dgoal_in.shape[0] // pieces
+    for number in range(pieces):
+        span = pl.ds(number * tall, tall)
+        pairs.append((dgoal_in.at[span, :], dgoal_out.at[span, :]))
+    copies = [
+        pltpu.make_async_copy(src, dst, sems.at[number]) for number, (src, dst) in enumerate(pairs)
+    ]
+    for copy in copies:
+        copy.start()
+    for copy in copies:
+        copy.wait()
 
 
 def per_device(n_wide, goals, premises, counts, positives, cotangent):
@@ -291,27 +322,30 @@
     n_hi = n_wide // n_lo
     own_goals, width = goals.shape
     rows = premises.shape[0]
-    all_goals = counts.shape[0]
+    all_goals, slots = positives.shape
     half = n_wide * rows
     bf16, f32 = jnp.bfloat16, jnp.float32
     vmem = pl.BlockSpec(memory_space=pltpu.VMEM)
     anywhere = pl.BlockSpec(memory_space=pl.ANY)
     dma = pltpu.SemaphoreType.DMA
+    limit = (16 if half <= 512 else 56) * 1024 * 1024
     scratch = [
         pltpu.VMEM((own_goals, width), f32),
         pltpu.VMEM((rows, width), f32),
+        pltpu.VMEM((1, all_goals), jnp.int32),
+        pltpu.VMEM((slots, all_goals), jnp.int32),
+        pltpu.VMEM((1, all_goals), f32),
         pltpu.VMEM((all_goals, width), bf16),
         pltpu.VMEM((2 * half, width), bf16),
         pltpu.VMEM((2 * half, all_goals), f32),
         pltpu.VMEM((2 * half, all_goals), f32),
         pltpu.VMEM((2 * half, all_goals), bf16),
-        pltpu.VMEM((own_goals, width), f32),
         pltpu.VMEM((half, width), f32),
         pltpu.VMEM((half, width), bf16),
         pltpu.VMEM((n_wide, rows, width), bf16),
         pltpu.VMEM((n_hi, rows, width), bf16),
         pltpu.VMEM((n_hi, rows, width), bf16),
-        dma((3,)),
+        dma((5,)),
         dma((2,)),
         dma((n_wide,)),
         dma((n_wide,)),
@@ -322,20 +356,43 @@
         dma((n_hi,)),
         dma((n_hi,)),
     ]
+    found = pl.pallas_call(
+        functools.partial(kernel, n_hi, n_lo),
+        out_shape=(
+            pltpu.VMEM((1, all_goals), f32),
+            pltpu.VMEM((own_goals, width), f32),
+            pltpu.VMEM((rows, width), f32),
+        ),
+        in_specs=[pl.BlockSpec(memory_space=pltpu.HBM)] * 5,
+        out_specs=(vmem, vmem, vmem),
+        scratch_shapes=scratch,
+        compiler_params=pltpu.CompilerParams(
+            collective_id=0, has_side_effects=True, vmem_limit_bytes=limit
+        ),
+    )(
+        *[
+            pltpu.with_memory_space_constraint(x, pltpu.HBM)
+            for x in (
+                goals,
+                premises,
+                counts.reshape(1, all_goals),
+                positives.T,
+                cotangent.reshape(1, all_goals),
+            )
+        ]
+    )
     loss, dgoal, dprem = pl.pallas_call(
-        functools.partial(kernel, n_hi, n_lo),
+        publish,
         out_shape=(
             jax.ShapeDtypeStruct((1, all_goals), f32),
             jax.ShapeDtypeStruct((own_goals, width), f32),
             jax.ShapeDtypeStruct((rows, width), f32),
         ),
-        in_specs=[anywhere, anywhere, vmem, vmem, vmem],
-        out_specs=(vmem, anywhere, vmem),
-        scratch_shapes=scratch,
-        compiler_params=pltpu.CompilerParams(
-            collective_id=0, has_side_effects=True, vmem_limit_bytes=58 * 1024 * 1024
-        ),
-    )(goals, premises, counts.reshape(1, all_goals), positives.T, cotangent.reshape(1, all_goals))
+        in_specs=[vmem] * 3,
+        out_specs=(anywhere,) * 3,
+        scratch_shapes=[dma((6,))],
+        compiler_params=pltpu.CompilerParams(has_side_effects=True),
+    )(*[pltpu.with_memory_space_constraint(x, pltpu.VMEM) for x in found])
     return (loss.reshape(all_goals), dgoal, dprem)
 
 

time: 36.8 us -> 30.4 us (0.83)
  local copies, waits for them, and re-layouts: 4.25 us -> 0 us
  Pallas kernels: 31.7 us -> 29.6 us
    unnamed x7 -> x0, local copies, waits for them, and re-layouts: 4.25 us -> none
    pallas_call x1 -> x2, Pallas kernels: 31.7 us -> 29.6 us  [the longest x1 28.6 us: per_device(): pl.pallas_call(functools.partial(kernel, n_hi, n_lo), out_shape=(pltpu.VM...]
where the time goes in v2:
time: 30.4 us; the launch traced here: 30.3 us
  Pallas kernels  29.6 us (97%)
  between operations  0.64 us (2%)
    pallas_call x1, Pallas kernels, per_device(): pl.pallas_call(functools.partial(kernel, n_hi, n_lo), out_shape=(pltpu.VM...  28.6 us
    pallas_call x1, Pallas kernels, per_device(): pl.pallas_call(publish, out_shape=(jax.ShapeDtypeStruct((1, all_goals), f...  1.06 us

profile of v2, /device:TPU:0, one launch (start us, length us, event | category | flops | bytes accessed | tf_op | source)
XLA Modules:
  0.0 30.3 jit_solution(1429855942427069098)
XLA Ops:
  0.6 28.6 %shard_map.76 = (f32[1,512]{1,0:T(1,128)S(1)}, f32[256,1024]{1,0:T(8,128)S(1)}, f32[32,1024]{1,0:T(8,128)S(1)}) custom-call(f32[256,1024]{1,0:T(8,128)} %goals_hbm.1, f32[32,1024]{1,0:T(8,128)} %prem_hbm.1, s32[1,512]{1,0:T(1,128)} %bitcast.5, s32[16,512]{1,0:T(8,128)} %bitcast.4, f32[1,512]{1,0:T(1,128)} %bitcast.6), custom_call_target="tpu_custom_call" | custom-call | tf_op jit(solution)/shard_map/pallas_call | solution.py:359
  29.2 1.1 %shard_map.77 = (f32[1,512]{1,0:T(1,128)}, f32[256,1024]{1,0:T(8,128)}, f32[32,1024]{1,0:T(8,128)}) custom-call(f32[1,512]{1,0:T(1,128)S(1)} %get-tuple-element.9.loss_in, f32[256,1024]{1,0:T(8,128)S(1)} %get-tuple-element.10.dgoal_in, f32[32,1024]{1,0:T(8,128)S(1)} %get-tuple-element.11.dprem_in), custom_call_target="tpu_custom_call" | custom-call | tf_op jit(solution)/shard_map/pallas_call | solution.py:384

commit v3 on v2

--- a/solution.py
+++ b/solution.py
@@ -13,6 +13,7 @@
 def kernel(
     n_hi,
     n_lo,
+    cuts,
     goals_hbm,
     prem_hbm,
     counts_hbm,
@@ -56,6 +57,7 @@
     rows, width = prem_in.shape
     own_goals = goals_in.shape[0]
     half = n_wide * rows
+    short = rows // cuts
     scale = width ** (-0.5)
 
     def hi_peer(a):
@@ -68,7 +70,8 @@
     if n_hi == 4:
         near_first = [1 + 2 * odd, 3 - 2 * odd, 2]
         arrive_first = [3 - 2 * odd, 1 + 2 * odd, 2]
-        far_first = [2, 3 - 2 * odd, 1 + 2 * odd]
+        first = 3 - 2 * odd
+        far_first = [2 + narrow * (first - 2), first + narrow * (2 - first), 1 + 2 * odd]
     else:
         near_first = arrive_first = far_first = list(range(1, n_hi))
 
@@ -94,39 +97,39 @@
     for load in small_loads:
         load.start()
 
-    def block(owner_wide, part):
-        start = pl.multiple_of(part * half + owner_wide * rows, rows)
-        return prem_all.at[pl.ds(start, rows), :]
+    def block(owner_wide, part, c):
+        start = pl.multiple_of(part * half + owner_wide * rows + c * short, short)
+        return prem_all.at[pl.ds(start, short), :]
 
     def source(a, b):
         return ((hi + n_hi - a) % n_hi) * n_lo + (lo + n_lo - b) % n_lo
 
-    def hi_copy(a, owner):
+    def hi_copy(a, owner, c):
         return pltpu.make_async_remote_copy(
-            src_ref=block(owner, 0),
-            dst_ref=block(owner, 0),
-            send_sem=ag_send.at[a * n_lo],
-            recv_sem=ag_recv.at[a * n_lo],
+            src_ref=block(owner, 0, c),
+            dst_ref=block(owner, 0, c),
+            send_sem=ag_send.at[a * n_lo * cuts + c],
+            recv_sem=ag_recv.at[a * n_lo * cuts + c],
             device_id=at(hi_peer(a), narrow),
             device_id_type=MESH,
         )
 
-    def lo_copy(a, b, owner):
+    def lo_copy(a, b, owner, c):
         return pltpu.make_async_remote_copy(
-            src_ref=block(owner, 0),
-            dst_ref=block(owner, 0),
-            send_sem=ag_send.at[a * n_lo + b],
-            recv_sem=ag_recv.at[a * n_lo + b],
+            src_ref=block(owner, 0, c),
+            dst_ref=block(owner, 0, c),
+            send_sem=ag_send.at[(a * n_lo + b) * cuts + c],
+            recv_sem=ag_recv.at[(a * n_lo + b) * cuts + c],
             device_id=at(lo_peer(b), narrow),
             device_id_type=MESH,
         )
 
-    def forward(a, b, owner):
+    def forward(a, b, owner, c):
         return pltpu.make_async_remote_copy(
-            src_ref=block(owner, 0),
-            dst_ref=block(owner, 1),
-            send_sem=fwd_send.at[a * n_lo + b],
-            recv_sem=fwd_recv.at[a * n_lo + b],
+            src_ref=block(owner, 0, c),
+            dst_ref=block(owner, 1, c),
+            send_sem=fwd_send.at[(a * n_lo + b) * cuts + c],
+            recv_sem=fwd_recv.at[(a * n_lo + b) * cuts + c],
             device_id=at(wide, 1 - narrow),
             device_id_type=MESH,
         )
@@ -134,11 +137,14 @@
     load_prem.wait()
     prem_all[pl.ds(pl.multiple_of(wide * rows, rows), rows), :] = prem_in[...].astype(jnp.bfloat16)
     pl.semaphore_wait(barrier, n_hi - 1 + n_lo - 1 + 1)
-    for b in range(1, n_lo):
-        lo_copy(0, b, wide).start()
+    for c in range(cuts):
+        for b in range(1, n_lo):
+            lo_copy(0, b, wide, c).start()
     for a in near_first:
-        hi_copy(a, wide).start()
-    forward(0, 0, wide).start()
+        for c in range(cuts):
+            hi_copy(a, wide, c).start()
+    for c in range(cuts):
+        forward(0, 0, wide, c).start()
 
     load_goals.wait()
     own_rows = pl.ds(pl.multiple_of(narrow * own_goals, own_goals), own_goals)
@@ -177,16 +183,18 @@
     lax.fori_loop(0, 2 * half // step, weigh, 0)
 
     for a in arrive_first:
-        owner = source(a, 0)
-        hi_copy(a, owner).wait_recv()
-        for b in range(1, n_lo):
-            lo_copy(a, b, owner).start()
-        forward(a, 0, owner).start()
+        for c in range(cuts):
+            owner = source(a, 0)
+            hi_copy(a, owner, c).wait_recv()
+            for b in range(1, n_lo):
+                lo_copy(a, b, owner, c).start()
+            forward(a, 0, owner, c).start()
     for a in [0] + arrive_first:
-        for b in range(1, n_lo):
-            owner = source(a, b)
-            lo_copy(a, b, owner).wait_recv()
-            forward(a, b, owner).start()
+        for c in range(cuts):
+            for b in range(1, n_lo):
+                owner = source(a, b)
+                lo_copy(a, b, owner, c).wait_recv()
+                forward(a, b, owner, c).start()
     goal_copy.wait()
 
     tall = min(256, half)
@@ -206,10 +214,11 @@
     pl.loop(0, half // tall)(lambda number: score(number * tall))
     for a in range(n_hi):
         for b in range(n_lo):
-            forward(a, b, source(a, b)).wait_recv()
+            for c in range(cuts):
+                forward(a, b, source(a, b), c).wait_recv()
     pl.loop(0, half // tall)(lambda number: score(half + number * tall))
 
-    lanes = 128
+    lanes = min(256 if half <= 512 else 128, all_goals)
 
     def soften(number, carry):
         cols = pl.ds(pl.multiple_of(number * lanes, lanes), lanes)
@@ -234,45 +243,49 @@
 
     pl.loop(0, half // tall)(premise_gradient)
 
-    def lo_reduce(a, b):
-        target_hi = (hi + a) % n_hi
-        target = target_hi * n_lo + (lo + b) % n_lo
+    def lo_reduce(a, b, c):
+        target = (hi + a) % n_hi * n_lo + (lo + b) % n_lo
+        start = pl.multiple_of(target * rows + c * short, short)
         return pltpu.make_async_remote_copy(
-            src_ref=lo_out.at[pl.ds(pl.multiple_of(target * rows, rows), rows), :],
-            dst_ref=lo_in.at[a * n_lo + b],
-            send_sem=lo_send.at[a * n_lo + b],
-            recv_sem=lo_recv.at[a * n_lo + b],
+            src_ref=lo_out.at[pl.ds(start, short), :],
+            dst_ref=lo_in.at[a * n_lo + b, pl.ds(c * short, short), :],
+            send_sem=lo_send.at[(a * n_lo + b) * cuts + c],
+            recv_sem=lo_recv.at[(a * n_lo + b) * cuts + c],
             device_id=at(lo_peer(b), narrow),
             device_id_type=MESH,
         )
 
-    def hi_reduce(a):
+    def hi_reduce(a, c):
         return pltpu.make_async_remote_copy(
-            src_ref=hi_out.at[a],
-            dst_ref=hi_in.at[a],
-            send_sem=hi_send.at[a],
-            recv_sem=hi_recv.at[a],
+            src_ref=hi_out.at[a, pl.ds(c * short, short), :],
+            dst_ref=hi_in.at[a, pl.ds(c * short, short), :],
+            send_sem=hi_send.at[a * cuts + c],
+            recv_sem=hi_recv.at[a * cuts + c],
             device_id=at(hi_peer(a), narrow),
             device_id_type=MESH,
         )
 
     for a in far_first + [0]:
+        for c in range(cuts):
+            for b in range(1, n_lo):
+                lo_reduce(a, b, c).start()
+
+    def pair_sum(a, c):
+        start = pl.multiple_of(hi_peer(a) * rows + c * short, short)
+        total = dprem[pl.ds(start, short), :]
         for b in range(1, n_lo):
-            lo_reduce(a, b).start()
-
-    def pair_sum(a):
-        target = hi_peer(a)
-        total = dprem[pl.ds(pl.multiple_of(target * rows, rows), rows), :]
-        for b in range(1, n_lo):
-            lo_reduce(a, b).wait_recv()
-            total = total + lo_in[a * n_lo + b].astype(jnp.float32)
+            lo_reduce(a, b, c).wait_recv()
+            total = total + lo_in[a * n_lo + b, pl.ds(c * short, short), :].astype(jnp.float32)
         return total
 
+    def send_sums():
+        for a in far_first:
+            for c in range(cuts):
+                hi_out[a, pl.ds(c * short, short), :] = pair_sum(a, c).astype(jnp.bfloat16)
+                hi_reduce(a, c).start()
+
     if n_lo == 1:
-        for a in range(1, n_hi):
-            hi_out[a] = pair_sum(a).astype(jnp.bfloat16)
-            hi_reduce(a).start()
-
+        send_sums()
     dgoal[...] = lax.dot_general(
         dscores[:, pl.ds(pl.multiple_of(narrow * own_goals, own_goals), own_goals)],
         prem_all[...],
@@ -281,24 +294,24 @@
     )
 
     if n_lo > 1:
-        for a in far_first:
-            hi_out[a] = pair_sum(a).astype(jnp.bfloat16)
-            hi_reduce(a).start()
-    mine = pair_sum(0)
-    for a in range(1, n_hi):
-        hi_reduce(a).wait_recv()
-        mine = mine + hi_in[a].astype(jnp.float32)
-    dprem_ref[...] = mine
-
-    for a in range(1, n_hi):
-        hi_copy(a, wide).wait_send()
-        hi_reduce(a).wait_send()
-    for a in range(n_hi):
-        for b in range(1, n_lo):
-            lo_copy(a, b, source(a, 0)).wait_send()
-            lo_reduce(a, b).wait_send()
-        for b in range(n_lo):
-            forward(a, b, source(a, b)).wait_send()
+        send_sums()
+    for c in range(cuts):
+        mine = pair_sum(0, c)
+        for a in range(1, n_hi):
+            hi_reduce(a, c).wait_recv()
+            mine = mine + hi_in[a, pl.ds(c * short, short), :].astype(jnp.float32)
+        dprem_ref[pl.ds(c * short, short), :] = mine
+
+    for c in range(cuts):
+        for a in range(1, n_hi):
+            hi_copy(a, wide, c).wait_send()
+            hi_reduce(a, c).wait_send()
+        for a in range(n_hi):
+            for b in range(1, n_lo):
+                lo_copy(a, b, source(a, 0), c).wait_send()
+                lo_reduce(a, b, c).wait_send()
+            for b in range(n_lo):
+                forward(a, b, source(a, b), c).wait_send()
 
 
 def publish(loss_in, dgoal_in, dprem_in, loss_out, dgoal_out, dprem_out, sems):
@@ -324,6 +337,7 @@
     rows = premises.shape[0]
     all_goals, slots = positives.shape
     half = n_wide * rows
+    cuts = 2 if rows % 32 == 0 else 1
     bf16, f32 = jnp.bfloat16, jnp.float32
     vmem = pl.BlockSpec(memory_space=pltpu.VMEM)
     anywhere = pl.BlockSpec(memory_space=pl.ANY)
@@ -347,17 +361,17 @@
         pltpu.VMEM((n_hi, rows, width), bf16),
         dma((5,)),
         dma((2,)),
-        dma((n_wide,)),
-        dma((n_wide,)),
-        dma((n_wide,)),
-        dma((n_wide,)),
-        dma((n_wide,)),
-        dma((n_wide,)),
-        dma((n_hi,)),
-        dma((n_hi,)),
+        dma((n_wide * cuts,)),
+        dma((n_wide * cuts,)),
+        dma((n_wide * cuts,)),
+        dma((n_wide * cuts,)),
+        dma((n_wide * cuts,)),
+        dma((n_wide * cuts,)),
+        dma((n_hi * cuts,)),
+        dma((n_hi * cuts,)),
     ]
     found = pl.pallas_call(
-        functools.partial(kernel, n_hi, n_lo),
+        functools.partial(kernel, n_hi, n_lo, cuts),
         out_shape=(
             pltpu.VMEM((1, all_goals), f32),
             pltpu.VMEM((own_goals, width), f32),

time: 30.4 us -> 29.7 us (0.977); the launches traced: 30.3 us -> 29.2 us
  Pallas kernels: 29.6 us -> 28.6 us
    pallas_call x1, Pallas kernels: 28.6 us -> 27.5 us  [per_device(): pl.pallas_call(functools.partial(kernel, n_hi, n_lo, cuts), out_shape=(pl...]
where the time goes in v3:
time: 29.7 us; the launch traced here: 29.2 us
  Pallas kernels  28.6 us (96%)
  between operations  0.64 us (2%)
    pallas_call x1, Pallas kernels, per_device(): pl.pallas_call(functools.partial(kernel, n_hi, n_lo, cuts), out_shape=(pl...  27.5 us
    pallas_call x1, Pallas kernels, per_device(): pl.pallas_call(publish, out_shape=(jax.ShapeDtypeStruct((1, all_goals), f...  1.06 us

profile of v3, /device:TPU:0, one launch (start us, length us, event | category | flops | bytes accessed | tf_op | source)
XLA Modules:
  0.0 29.2 jit_solution(4310935053251129032)
XLA Ops:
  0.6 27.5 %shard_map.76 = (f32[1,512]{1,0:T(1,128)S(1)}, f32[256,1024]{1,0:T(8,128)S(1)}, f32[32,1024]{1,0:T(8,128)S(1)}) custom-call(f32[256,1024]{1,0:T(8,128)} %goals_hbm.1, f32[32,1024]{1,0:T(8,128)} %prem_hbm.1, s32[1,512]{1,0:T(1,128)} %bitcast.5, s32[16,512]{1,0:T(8,128)} %bitcast.4, f32[1,512]{1,0:T(1,128)} %bitcast.6), custom_call_target="tpu_custom_call" | custom-call | tf_op jit(solution)/shard_map/pallas_call | solution.py:373
  28.2 1.1 %shard_map.77 = (f32[1,512]{1,0:T(1,128)}, f32[256,1024]{1,0:T(8,128)}, f32[32,1024]{1,0:T(8,128)}) custom-call(f32[1,512]{1,0:T(1,128)S(1)} %get-tuple-element.9.loss_in, f32[256,1024]{1,0:T(8,128)S(1)} %get-tuple-element.10.dgoal_in, f32[32,1024]{1,0:T(8,128)S(1)} %get-tuple-element.11.dprem_in), custom_call_target="tpu_custom_call" | custom-call | tf_op jit(solution)/shard_map/pallas_call | solution.py:398

commit v4 on v3

--- a/solution.py
+++ b/solution.py
@@ -68,8 +68,10 @@
 
     odd = hi % 2
     if n_hi == 4:
-        near_first = [1 + 2 * odd, 3 - 2 * odd, 2]
-        arrive_first = [3 - 2 * odd, 1 + 2 * odd, 2]
+        cross = 3 - 2 * odd
+        near_first = [1 + 2 * odd, cross + narrow * (2 - cross), 2 + narrow * (cross - 2)]
+        late = 1 + 2 * odd
+        arrive_first = [3 - 2 * odd, late + narrow * (2 - late), 2 + narrow * (late - 2)]
         first = 3 - 2 * odd
         far_first = [2 + narrow * (first - 2), first + narrow * (2 - first), 1 + 2 * odd]
     else:
@@ -316,7 +318,7 @@
 
 def publish(loss_in, dgoal_in, dprem_in, loss_out, dgoal_out, dprem_out, sems):
     pairs = [(loss_in, loss_out), (dprem_in, dprem_out)]
-    pieces = 4
+    pieces = 1
     tall = dgoal_in.shape[0] // pieces
     for number in range(pieces):
         span = pl.ds(number * tall, tall)
@@ -404,7 +406,7 @@
         ),
         in_specs=[vmem] * 3,
         out_specs=(anywhere,) * 3,
-        scratch_shapes=[dma((6,))],
+        scratch_shapes=[dma((3,))],
         compiler_params=pltpu.CompilerParams(has_side_effects=True),
     )(*[pltpu.with_memory_space_constraint(x, pltpu.VMEM) for x in found])
     return (loss.reshape(all_goals), dgoal, dprem)

time: 29.7 us -> 29.7 us (level)
  no operation moved by 1% of the time
where the time goes in v4:
time: 29.7 us; the launch traced here: 29.2 us
  Pallas kernels  28.6 us (96%)
  between operations  0.64 us (2%)
    pallas_call x1, Pallas kernels, per_device(): pl.pallas_call(functools.partial(kernel, n_hi, n_lo, cuts), out_shape=(pl...  27.5 us
    pallas_call x1, Pallas kernels, per_device(): pl.pallas_call(publish, out_shape=(jax.ShapeDtypeStruct((1, all_goals), f...  1.05 us

profile of v4, /device:TPU:0, one launch (start us, length us, event | category | flops | bytes accessed | tf_op | source)
XLA Modules:
  0.0 29.2 jit_solution(3289938484102105523)
XLA Ops:
  0.6 27.5 %shard_map.76 = (f32[1,512]{1,0:T(1,128)S(1)}, f32[256,1024]{1,0:T(8,128)S(1)}, f32[32,1024]{1,0:T(8,128)S(1)}) custom-call(f32[256,1024]{1,0:T(8,128)} %goals_hbm.1, f32[32,1024]{1,0:T(8,128)} %prem_hbm.1, s32[1,512]{1,0:T(1,128)} %bitcast.5, s32[16,512]{1,0:T(8,128)} %bitcast.4, f32[1,512]{1,0:T(1,128)} %bitcast.6), custom_call_target="tpu_custom_call" | custom-call | tf_op jit(solution)/shard_map/pallas_call | solution.py:375
  28.2 1.0 %shard_map.77 = (f32[1,512]{1,0:T(1,128)}, f32[256,1024]{1,0:T(8,128)}, f32[32,1024]{1,0:T(8,128)}) custom-call(f32[1,512]{1,0:T(1,128)S(1)} %get-tuple-element.9.loss_in, f32[256,1024]{1,0:T(8,128)S(1)} %get-tuple-element.10.dgoal_in, f32[32,1024]{1,0:T(8,128)S(1)} %get-tuple-element.11.dprem_in), custom_call_target="tpu_custom_call" | custom-call | tf_op jit(solution)/shard_map/pallas_call | solution.py:400
